TPU v7x, 256 devices: a whole 4x4x8 slice. The times are simulated.
256 devices in a mesh: seg: 8 (over y, core), ep: 32 (over z, x).
Axes of the slice: x: 4, y: 4, z: 8, core: 2. Of those that a mesh axis runs over, the one named last changes fastest.
Arguments:
- queries: bfloat16 [16384, 8192], P(('seg', 'ep')), may hold values from -6 to 6
- keys: bfloat16 [16384, 8192], P(('seg', 'ep')), may hold values from -1.25 to 1.25
- values: bfloat16 [16384, 8192], P(('seg', 'ep')), may hold values from -54 to 54
- log_decay: float32 [16384, 64], P('seg', 'ep'), may hold values from -1 to 0
- out_gain: float32 [8192], replicated, may hold values from 0.1 to 1.9
- out_proj: bfloat16 [8192, 6144], P('ep', 'seg'), may hold values from -0.0625 to 0.0625
- experts: int32 [2048, 2], P(('seg', 'ep')), may hold values from 0 to 15, all different within a row; in each aligned block of 8 rows (0 to 7, 8 to 15, ...) at most 2 rows name the same one
- gates: float32 [2048, 2], P(('seg', 'ep')), may hold values from 0.2 to 1
- up_weight: bfloat16 [32, 6144, 2304], P('ep', None, 'seg'), may hold values from -0.078125 to 0.078125
- down_weight: bfloat16 [32, 2304, 6144], P('ep', 'seg'), may hold values from -0.09375 to 0.09375
Outputs:
- attn_out: bfloat16 [16384, 8192], P(('seg', 'ep'))
- moe_out: bfloat16 [2048, 6144], P(('seg', 'ep'))
Inputs may be any that keep to these rules, and one draw needn't show every extreme that they name: Each row names two different experts. The 8 rows of one device name any one expert at most 2 times, and in some devices one expert exactly 2 times.
All inputs are finite; a program needn't handle non-finite values.
Results may differ from a plain program's by a relative error of at most 0.025.
Values may be sent and summed in bfloat16 or wider, within the bound.
No kernel may reach another device: no remote copies, remote signals or barrier semaphores. Data moves between devices by JAX's collectives and lax.ppermute only.
A program may use at most 128 MiB of HBM per device.

v0:
```python
import math
import jax
import jax.numpy as jnp
from jax import lax
from jax.sharding import Mesh
from jax.sharding import PartitionSpec as P

EP = ("ep_0", "ep_1")
SEG_EP = ("seg", "ep_0", "ep_1")
epsilon = 1e-06


def side_by_side(arrays, axis, dim, along):
    columns = [a.reshape(*a.shape[:along], -1) for a in arrays]
    both = jnp.concatenate(columns, axis=along)
    whole, at, done = (lax.all_gather(both, axis, axis=dim, tiled=True), 0, [])
    for a, column in zip(arrays, columns):
        section = whole[..., at : at + column.shape[along]]
        done.append(section.reshape(*section.shape[:along], *a.shape[along:]))
        at += column.shape[along]
    return tuple(done)


def sent_to_all(x, axis):
    devices = lax.axis_size(axis)
    return lax.all_to_all(jnp.broadcast_to(x[None], (devices, *x.shape)), axis, 0, 0, tiled=True)


def taken_together(x, axis):
    return sent_to_all(x, axis).sum(axis=0)


def scatter_axes(x, axes, dim):
    for axis in axes:
        x = lax.psum_scatter(x, axis, scatter_dimension=dim, tiled=True)
    return x


def route_tables(experts, gates, expert_count, capacity):
    token_count = experts.shape[0]
    flattened = experts.reshape(-1)
    onehot = (flattened[:, None] == jnp.arange(expert_count, dtype=jnp.int32)[None, :]).astype(
        jnp.int32
    )
    earlier = jnp.cumsum(onehot, axis=0) - onehot
    position = jnp.sum(earlier * onehot, axis=1)
    slot_index = (flattened * capacity + position).reshape(token_count, 2)
    columns = jnp.arange(expert_count * capacity, dtype=jnp.int32)
    matches = slot_index[:, :, None] == columns[None, None, :]
    dispatch = jnp.any(matches, axis=1).T.astype(jnp.bfloat16)
    combine = jnp.sum(jnp.where(matches, gates[:, :, None], 0.0), axis=1)
    return (dispatch, combine)


def expert_output(row_data, up_piece, down_piece):
    hidden = jax.nn.silu(jnp.dot(row_data, up_piece, preferred_element_type=jnp.float32)).astype(
        jnp.bfloat16
    )
    return jnp.dot(hidden, down_piece, preferred_element_type=jnp.float32)


def on_device(
    queries, keys, values, log_decay, out_gain, out_proj, experts, gates, up_weight, down_weight
):
    ep_count = lax.axis_size(EP)
    heads_local = log_decay.shape[1]
    head_dim = queries.shape[1] // (heads_local * ep_count)
    query_heads, key_heads, value_heads = (
        lax.all_to_all(queries, EP, split_axis=1, concat_axis=0, tiled=True),
        lax.all_to_all(keys, EP, split_axis=1, concat_axis=0, tiled=True),
        lax.all_to_all(values, EP, split_axis=1, concat_axis=0, tiled=True),
    )
    seg_length = query_heads.shape[0]
    query_heads = query_heads.reshape(seg_length, heads_local, head_dim)
    key_heads = key_heads.reshape(seg_length, heads_local, head_dim)
    value_heads = value_heads.reshape(seg_length, heads_local, head_dim)
    cumulative = jnp.cumsum(log_decay, axis=0)
    across = cumulative.T
    block_size = math.gcd(seg_length, 512)
    starts = jnp.arange(seg_length // block_size, dtype=jnp.int32) * block_size
    token_positions = jnp.arange(seg_length, dtype=jnp.int32)

    def block_mix(start):
        query_block = lax.dynamic_slice_in_dim(query_heads, start, block_size, 0)
        cum_block = lax.dynamic_slice_in_dim(across, start, block_size, 1)
        row_ids = start + jnp.arange(block_size, dtype=jnp.int32)
        causal = (row_ids[:, None] >= token_positions[None, :])[None]
        log_gap = cum_block[:, :, None] - across[:, None, :]
        weight = jnp.where(causal, jnp.exp(jnp.where(causal, log_gap, 0.0)), 0.0)
        scores = jnp.einsum(
            "thd,shd->hts", query_block, key_heads, preferred_element_type=jnp.float32
        )
        mixing = (scores * weight).astype(jnp.bfloat16)
        return jnp.einsum("hts,she->the", mixing, value_heads, preferred_element_type=jnp.float32)

    inside = lax.map(block_mix, starts).reshape(seg_length, heads_local, head_dim)
    ending = cumulative[-1]
    to_end = jnp.exp(ending[None, :] - cumulative)
    key_float = key_heads.astype(jnp.float32)
    value_float = value_heads.astype(jnp.float32)
    local_state = jnp.einsum("sh,shd,she->hde", to_end, key_float, value_float)
    all_ends, all_states = tuple(
        (
            part.astype(jnp.float32)
            for part in side_by_side(
                (ending[None].astype(jnp.bfloat16), local_state[None].astype(jnp.bfloat16)),
                "seg",
                0,
                2,
            )
        )
    )
    own_group = lax.axis_index("seg")
    group_ids = jnp.arange(all_ends.shape[0], dtype=jnp.int32)
    before = (group_ids < own_group)[:, None]
    through = jnp.cumsum(all_ends, axis=0)
    reaching = jnp.sum(jnp.where(before, all_ends, 0.0), axis=0)
    factors = jnp.where(before, jnp.exp(jnp.where(before, reaching[None, :] - through, 0.0)), 0.0)
    carried = jnp.einsum("gh,ghde->hde", factors, all_states)
    outside = jnp.exp(cumulative)[:, :, None] * jnp.einsum(
        "thd,hde->the", query_heads.astype(jnp.float32), carried
    )
    mixture = (inside + outside).astype(jnp.bfloat16).reshape(seg_length, heads_local * head_dim)
    token_mix = lax.all_to_all(mixture, EP, split_axis=0, concat_axis=1, tiled=True)
    as_float = token_mix.astype(jnp.float32)
    inv_rms = lax.rsqrt(jnp.mean(as_float * as_float, axis=1, keepdims=True) + epsilon)
    attn_out = (as_float * inv_rms * out_gain[None, :]).astype(jnp.bfloat16)
    row_stride = 8
    own_width = heads_local * head_dim
    feature_count = own_width * ep_count
    picked_float = mixture.reshape(seg_length // row_stride, row_stride, own_width)[:, 0].astype(
        jnp.float32
    )
    square_sums = taken_together(jnp.sum(picked_float * picked_float, axis=1), EP)
    picked_rms = lax.rsqrt(square_sums[:, None] / feature_count + epsilon)
    gain_slice = lax.dynamic_slice_in_dim(out_gain, lax.axis_index(EP) * own_width, own_width, 0)
    normed_rows = (picked_float * picked_rms * gain_slice[None, :]).astype(jnp.bfloat16)
    proj_terms = jnp.dot(
        normed_rows,
        lax.all_gather(out_proj, "seg", axis=1, tiled=True),
        preferred_element_type=jnp.float32,
    )
    moe_in = (
        scatter_axes(proj_terms.astype(jnp.bfloat16), EP, 0)
        .astype(jnp.float32)
        .astype(jnp.bfloat16)
    )
    expert_count = ep_count // 2
    token_count, model_width = moe_in.shape
    capacity = max(2, 4 * token_count // expert_count)
    dispatch, combine = route_tables(experts, gates, expert_count, capacity)
    up_piece = up_weight[0]
    down_piece = down_weight[0]
    slot_rows = jnp.dot(dispatch, moe_in, preferred_element_type=jnp.float32).astype(jnp.bfloat16)
    outgoing = jnp.repeat(slot_rows.reshape(expert_count, capacity, model_width), 2, axis=0)
    arrived = lax.all_to_all(outgoing, EP, split_axis=0, concat_axis=0, tiled=True).reshape(
        ep_count * capacity, model_width
    )
    gathered = lax.all_gather(arrived, "seg", axis=0, tiled=True)
    owned_sums = lax.psum_scatter(
        expert_output(gathered, up_piece, down_piece).astype(jnp.bfloat16),
        "seg",
        scatter_dimension=0,
        tiled=True,
    ).astype(jnp.float32)
    returned_back = lax.all_to_all(
        owned_sums.reshape(ep_count, capacity, model_width).astype(jnp.bfloat16),
        EP,
        split_axis=0,
        concat_axis=0,
        tiled=True,
    ).astype(jnp.float32)
    paired = returned_back.reshape(expert_count, 2, capacity, model_width)
    halves = (paired[:, 0] + paired[:, 1]).reshape(expert_count * capacity, model_width)
    summed = jnp.dot(combine, halves)
    moe_out = summed.astype(jnp.bfloat16)
    return (attn_out, moe_out)


def solution(mesh):
    torus = Mesh(mesh.devices.reshape(mesh.shape["seg"], 8, 4), ("seg", "ep_0", "ep_1"))
    placed = (
        P(SEG_EP, None),
        P(SEG_EP, None),
        P(SEG_EP, None),
        P("seg", EP),
        P(),
        P(EP, "seg"),
        P(SEG_EP, None),
        P(SEG_EP, None),
        P(EP, None, "seg"),
        P(EP, "seg", None),
    )
    return jax.shard_map(
        on_device,
        mesh=torus,
        in_specs=placed,
        out_specs=(P(SEG_EP, None), P(SEG_EP, None)),
        check_vma=False,
    )
```

profile of v0, /device:TPU:2, one launch (start us, length us, event | category | flops | bytes accessed | tf_op | source)
XLA Modules:
  0.0 520.2 jit_solution(4376102759249833830)
XLA Ops:
  7.2 2.5 copy.199
  9.7 11.8 %all-to-all-start.1 = ((bf16[64,32,256]{2,0,1:T(8,128)(2,1)}), bf16[64,32,256]{2,0,1:T(8,128)(2,1)}, u32[]{:S(2)}, u32[]{:S(2)}) async-start(bf16[64,32,256]{2,0,1:T(8,128)(2,1)} %bitcast.112), calls=%async_computation.1 | async-start | bytes 2097152 | tf_op jit(solution)/shard_map/all_to_all | solution.py:70
  21.5 2.3 copy.198
  23.8 25.8 %all-to-all-done.1 = bf16[64,32,256]{2,0,1:T(8,128)(2,1)} async-done(((bf16[64,32,256]{2,0,1:T(8,128)(2,1)}), bf16[64,32,256]{2,0,1:T(8,128)(2,1)}, u32[]{:S(2)}, u32[]{:S(2)}) %all-to-all-start.1) | async-done | bytes 1048608 | tf_op jit(solution)/shard_map/all_to_all | solution.py:70
  49.6 5.6 %all-to-all-start.2 = ((bf16[64,32,256]{2,0,1:T(8,128)(2,1)}), bf16[64,32,256]{2,0,1:T(8,128)(2,1)}, u32[]{:S(2)}, u32[]{:S(2)}) async-start(bf16[64,32,256]{2,0,1:T(8,128)(2,1)} %bitcast.110), calls=%async_computation.2 | async-start | bytes 2097152 | tf_op jit(solution)/shard_map/all_to_all | solution.py:71
  64.1 2.3 copy.200
  67.8 2.2 reshape.156
  70.0 12.2 %all-to-all-done.2 = bf16[64,32,256]{2,0,1:T(8,128)(2,1)} async-done(((bf16[64,32,256]{2,0,1:T(8,128)(2,1)}), bf16[64,32,256]{2,0,1:T(8,128)(2,1)}, u32[]{:S(2)}, u32[]{:S(2)}) %all-to-all-start.2) | async-done | bytes 1048608 | tf_op jit(solution)/shard_map/all_to_all | solution.py:71
  82.3 5.6 %all-to-all-start = ((bf16[64,32,256]{2,0,1:T(8,128)(2,1)}), bf16[64,32,256]{2,0,1:T(8,128)(2,1)}, u32[]{:S(2)}, u32[]{:S(2)}) async-start(bf16[64,32,256]{2,0,1:T(8,128)(2,1)} %bitcast.111), calls=%async_computation | async-start | bytes 2097152 | tf_op jit(solution)/shard_map/all_to_all | solution.py:69
  87.9 2.2 reshape.159
  90.1 5.6 %convert_multiply_fusion.1 = bf16[2048,2,128]{2,1,0:T(2,128)(2,1)S(1)} fusion(bf16[2048,2,128]{2,1,0:T(2,128)(2,1)} %reshape.156, f32[2048,2]{1,0:T(8,128)} %copy.139), kind=kLoop, calls=%fused_computation.27 | loop fusion | flops 1572864 | bytes 2113536 | tf_op jit(solution)/shard_map/sh,shd,she->hde/dot_general | solution.py:101
  95.7 2.5 fusion.18
  100.7 13.8 %all_gather.9 = bf16[8,2,16385]{2,1,0:T(2,128)(2,1)S(1)} all-gather(bf16[1,2,16385]{2,1,0:T(2,128)(2,1)S(1)} %pad_maximum_fusion), channel_id=1, replica_groups=mesh['seg'=8,'ep_0'=8,'ep_1'=4] {'seg'}, dimensions={0}, use_global_device_ids=true | all-gather | bytes 589860 | tf_op jit(solution)/shard_map/all_gather | solution.py:16
  116.0 2.4 copy.136
  120.3 2.2 reshape.163
  122.6 2.1 reshape.155
  124.7 2.3 copy.135
  127.0 99.5 %while.11 = (s32[]{:T(128)}, f32[4,512,2,128]{1,0,3,2:T(4,128)}, s32[4]{0:T(128)S(1)}, bf16[2048,2,128]{2,0,1:T(8,128)(2,1)}, bf16[2048,2,128]{2,0,1:T(8,128)(2,...) while((s32[]{:T(128)}, f32[4,512,2,128]{1,0,3,2:T(4,128)}, ...), condition=%wide.region_3.4_spmd.clone, body=%wide.region_2.3_spmd.clone.sunk | while | flops 1085276672 | bytes 7110819 | solution.py:96
  132.3 6.6 %fusion.58 = f32[1,512,2,128]{3,1,2,0:T(8,128)} fusion(bf16[2048,2,128]{2,0,1:T(8,128)(2,1)} %get-tuple-element.204, bf16[2048,2,128]{2,0,1:T(8,128)(2,1)} %get-tuple-element.202, f32[2,2048]{1,0:T(2,128)} %get-tuple-element.203, f32[2,512]{1,0:T(2,128)S(1)} %constant_dynamic-slice_fusion.2, pred[512,2048]{1,0:T(8,128)(4,1)} %iota_compare_fusion.5, ...), kind=kOutput, calls=%fused_computation.4.clone.1 | convolution fusion | flops 1084227584 | bytes 3952644 | tf_op jit(solution)/shard_map/while/body/eval_jaxpr/hts,she->the/dot_general | solution.py:94
  140.8 11.1 %dynamic_update_slice.6 = f32[4,512,2,128]{1,0,3,2:T(4,128)} dynamic-update-slice(f32[4,512,2,128]{1,0,3,2:T(4,128)} %get-tuple-element.189, f32[1,512,2,128]{1,0,3,2:T(1,128)} %copy.204, s32[]{:T(128)} %get-tuple-element.188, s32[]{:T(128)} %constant.22.clone.1..sunk, s32[]{:T(128)} %constant.22.clone.1..sunk, s32[]{:T(128)} %constant.22.clone.1..sunk) | dynamic-update-slice | bytes 1048580 | tf_op jit(solution)/shard_map/while/body/jit(dynamic_update_index_in_dim)/dynamic_update_slice | solution.py:96
  157.2 6.6 %fusion.58 = f32[1,512,2,128]{3,1,2,0:T(8,128)} fusion(bf16[2048,2,128]{2,0,1:T(8,128)(2,1)} %get-tuple-element.204, bf16[2048,2,128]{2,0,1:T(8,128)(2,1)} %get-tuple-element.202, f32[2,2048]{1,0:T(2,128)} %get-tuple-element.203, f32[2,512]{1,0:T(2,128)S(1)} %constant_dynamic-slice_fusion.2, pred[512,2048]{1,0:T(8,128)(4,1)} %iota_compare_fusion.5, ...), kind=kOutput, calls=%fused_computation.4.clone.1 | convolution fusion | flops 1084227584 | bytes 3952644 | tf_op jit(solution)/shard_map/while/body/eval_jaxpr/hts,she->the/dot_general | solution.py:94
  165.7 11.1 %dynamic_update_slice.6 = f32[4,512,2,128]{1,0,3,2:T(4,128)} dynamic-update-slice(f32[4,512,2,128]{1,0,3,2:T(4,128)} %get-tuple-element.189, f32[1,512,2,128]{1,0,3,2:T(1,128)} %copy.204, s32[]{:T(128)} %get-tuple-element.188, s32[]{:T(128)} %constant.22.clone.1..sunk, s32[]{:T(128)} %constant.22.clone.1..sunk, s32[]{:T(128)} %constant.22.clone.1..sunk) | dynamic-update-slice | bytes 1048580 | tf_op jit(solution)/shard_map/while/body/jit(dynamic_update_index_in_dim)/dynamic_update_slice | solution.py:96
  182.0 6.6 %fusion.58 = f32[1,512,2,128]{3,1,2,0:T(8,128)} fusion(bf16[2048,2,128]{2,0,1:T(8,128)(2,1)} %get-tuple-element.204, bf16[2048,2,128]{2,0,1:T(8,128)(2,1)} %get-tuple-element.202, f32[2,2048]{1,0:T(2,128)} %get-tuple-element.203, f32[2,512]{1,0:T(2,128)S(1)} %constant_dynamic-slice_fusion.2, pred[512,2048]{1,0:T(8,128)(4,1)} %iota_compare_fusion.5, ...), kind=kOutput, calls=%fused_computation.4.clone.1 | convolution fusion | flops 1084227584 | bytes 3952644 | tf_op jit(solution)/shard_map/while/body/eval_jaxpr/hts,she->the/dot_general | solution.py:94
  190.5 11.1 %dynamic_update_slice.6 = f32[4,512,2,128]{1,0,3,2:T(4,128)} dynamic-update-slice(f32[4,512,2,128]{1,0,3,2:T(4,128)} %get-tuple-element.189, f32[1,512,2,128]{1,0,3,2:T(1,128)} %copy.204, s32[]{:T(128)} %get-tuple-element.188, s32[]{:T(128)} %constant.22.clone.1..sunk, s32[]{:T(128)} %constant.22.clone.1..sunk, s32[]{:T(128)} %constant.22.clone.1..sunk) | dynamic-update-slice | bytes 1048580 | tf_op jit(solution)/shard_map/while/body/jit(dynamic_update_index_in_dim)/dynamic_update_slice | solution.py:96
  206.9 6.6 %fusion.58 = f32[1,512,2,128]{3,1,2,0:T(8,128)} fusion(bf16[2048,2,128]{2,0,1:T(8,128)(2,1)} %get-tuple-element.204, bf16[2048,2,128]{2,0,1:T(8,128)(2,1)} %get-tuple-element.202, f32[2,2048]{1,0:T(2,128)} %get-tuple-element.203, f32[2,512]{1,0:T(2,128)S(1)} %constant_dynamic-slice_fusion.2, pred[512,2048]{1,0:T(8,128)(4,1)} %iota_compare_fusion.5, ...), kind=kOutput, calls=%fused_computation.4.clone.1 | convolution fusion | flops 1084227584 | bytes 3952644 | tf_op jit(solution)/shard_map/while/body/eval_jaxpr/hts,she->the/dot_general | solution.py:94
  215.4 11.1 %dynamic_update_slice.6 = f32[4,512,2,128]{1,0,3,2:T(4,128)} dynamic-update-slice(f32[4,512,2,128]{1,0,3,2:T(4,128)} %get-tuple-element.189, f32[1,512,2,128]{1,0,3,2:T(1,128)} %copy.204, s32[]{:T(128)} %get-tuple-element.188, s32[]{:T(128)} %constant.22.clone.1..sunk, s32[]{:T(128)} %constant.22.clone.1..sunk, s32[]{:T(128)} %constant.22.clone.1..sunk) | dynamic-update-slice | bytes 1048580 | tf_op jit(solution)/shard_map/while/body/jit(dynamic_update_index_in_dim)/dynamic_update_slice | solution.py:96
  226.5 3.7 reshape.160
  233.2 3.4 fusion.14
  236.6 3.7 copy.145
  240.3 2.5 reshape_reshape.3
  245.6 9.8 %all-to-all-start.4 = ((f32[32,1,256]{2,1,0:T(1,128)}), f32[32,1,256]{2,1,0:T(1,128)}, u32[]{:S(2)}, u32[]{:S(2)}) async-start(f32[32,1,256]{2,1,0:T(1,128)} %broadcast_in_dim.85), calls=%async_computation.4 | async-start | bytes 65536 | tf_op jit(solution)/shard_map/all_to_all | solution.py:26
  256.3 7.8 %all-to-all-done.4 = f32[32,1,256]{2,1,0:T(1,128)} async-done(((f32[32,1,256]{2,1,0:T(1,128)}), f32[32,1,256]{2,1,0:T(1,128)}, u32[]{:S(2)}, u32[]{:S(2)}) %all-to-all-start.4) | async-done | bytes 32800 | tf_op jit(solution)/shard_map/all_to_all | solution.py:26
  265.0 4.7 convolution_convert_fusion.1
  269.8 41.9 %reduce-scatter.4.cloned.1.call-done = bf16[32,6144]{1,0:T(8,128)(2,1)} async-done(((bf16[256,6144]{1,0:T(8,128)(2,1)}), bf16[32,6144]{1,0:T(8,128)(2,1)}) %reduce-scatter.4.cloned.1.call-update) | async-done | bytes 393232 | tf_op jit(solution)/shard_map/reduce_scatter | solution.py:35
  315.2 19.9 %reduce-scatter.6.cloned.1.call-done = bf16[8,6144]{1,0:T(8,128)(2,1)} async-done(((bf16[32,6144]{1,0:T(8,128)(2,1)}), bf16[8,6144]{1,0:T(8,128)(2,1)}) %reduce-scatter.6.cloned.1.call-update) | async-done | bytes 98320 | tf_op jit(solution)/shard_map/reduce_scatter | solution.py:35
  337.0 2.0 reshape.164
  340.4 30.7 %all_to_all.77 = bf16[32,2,6144]{2,1,0:T(2,128)(2,1)} all-to-all(bf16[32,2,6144]{2,1,0:T(2,128)(2,1)S(1)} %bitcast.113), channel_id=1, replica_groups=mesh['seg'=8,'ep_0'=8,'ep_1'=4] {'ep_0','ep_1'}, dimensions={0} | all-to-all | bytes 1572864 | tf_op jit(solution)/shard_map/all_to_all | solution.py:156
  371.2 3.0 reshape.166
  374.2 40.3 %all-gather.5.cloned.1.call-done = bf16[512,6144]{1,0:T(8,128)(2,1)} async-done(((bf16[64,6144]{1,0:T(8,128)(2,1)}), bf16[512,6144]{1,0:T(8,128)(2,1)}) %all-gather.5.cloned.1.call-update) | async-done | bytes 6291472 | tf_op jit(solution)/shard_map/all_gather | solution.py:159
  414.5 12.0 %convolution_convert_fusion = bf16[512,6144]{1,0:T(8,128)(2,1)} fusion(bf16[1,288,6144]{2,1,0:T(8,128)(2,1)S(1)} %copy-done, bf16[512,6144]{1,0:T(8,128)(2,1)} %all-gather.5.cloned.1.call-done, bf16[1,6144,288]{1,2,0:T(8,128)(2,1)} %param.20), kind=kOutput, calls=%fused_computation.10 | convolution fusion | flops 3627761664 | bytes 19660800 | tf_op jit(solution)/shard_map/dot_general | solution.py:59
  426.6 2.5 all_to_all.65
  429.1 10.2 %all-to-all-start.3 = ((bf16[32,64,256]{2,1,0:T(8,128)(2,1)}), bf16[32,64,256]{2,1,0:T(8,128)(2,1)}, u32[]{:S(2)}, u32[]{:S(2)}) async-start(bf16[32,64,256]{2,1,0:T(8,128)(2,1)} %all_to_all.65), calls=%async_computation.3 | async-start | bytes 2097152 | tf_op jit(solution)/shard_map/all_to_all | solution.py:124
  439.4 28.5 %all-to-all-done.3 = bf16[32,64,256]{2,1,0:T(8,128)(2,1)} async-done(((bf16[32,64,256]{2,1,0:T(8,128)(2,1)}), bf16[32,64,256]{2,1,0:T(8,128)(2,1)}, u32[]{:S(2)}, u32[]{:S(2)}) %all-to-all-start.3) | async-done | bytes 1048608 | tf_op jit(solution)/shard_map/all_to_all | solution.py:124
  472.5 2.9 convert_element_type.93
  475.3 9.8 %all-to-all-start.6 = ((bf16[32,2,6144]{2,1,0:T(2,128)(2,1)}), bf16[32,2,6144]{2,1,0:T(2,128)(2,1)}, u32[]{:S(2)}, u32[]{:S(2)}) async-start(bf16[32,2,6144]{2,1,0:T(2,128)(2,1)} %convert_element_type.93), calls=%async_computation.9 | async-start | bytes 1572864 | tf_op jit(solution)/shard_map/all_to_all | solution.py:166
  485.2 2.8 multiply_convert_fusion.1
  488.0 18.8 %all-to-all-done.6 = bf16[32,2,6144]{2,1,0:T(2,128)(2,1)} async-done(((bf16[32,2,6144]{2,1,0:T(2,128)(2,1)}), bf16[32,2,6144]{2,1,0:T(2,128)(2,1)}, u32[]{:S(2)}, u32[]{:S(2)}) %all-to-all-start.6) | async-done | bytes 786464 | tf_op jit(solution)/shard_map/all_to_all | solution.py:166
  506.8 2.0 convert.7
  (98 shorter events, 62.2 us)
Async XLA Ops:
  7.2 407.3 %copy-start = (bf16[1,288,6144]{2,1,0:T(8,128)(2,1)S(1)}, bf16[1,288,6144]{2,1,0:T(8,128)(2,1)}, u32[]{:S(2)}) copy-start(bf16[1,288,6144]{2,1,0:T(8,128)(2,1)} %param.21) | copy-start | bytes 10616836
  9.7 46.3 %copy-start.4 = (f32[2048,2]{0,1:T(2,128)S(1)}, f32[2048,2]{0,1:T(2,128)}, u32[]{:S(2)}) copy-start(f32[2048,2]{0,1:T(2,128)} %param.15) | copy-start | bytes 49156
  9.7 39.9 %all-to-all-start.1 = ((bf16[64,32,256]{2,0,1:T(8,128)(2,1)}), bf16[64,32,256]{2,0,1:T(8,128)(2,1)}, u32[]{:S(2)}, u32[]{:S(2)}) async-start(bf16[64,32,256]{2,0,1:T(8,128)(2,1)} %bitcast.112), calls=%async_computation.1 | async-start | bytes 2097152 | tf_op jit(solution)/shard_map/all_to_all | solution.py:70
  49.6 32.7 %all-to-all-start.2 = ((bf16[64,32,256]{2,0,1:T(8,128)(2,1)}), bf16[64,32,256]{2,0,1:T(8,128)(2,1)}, u32[]{:S(2)}, u32[]{:S(2)}) async-start(bf16[64,32,256]{2,0,1:T(8,128)(2,1)} %bitcast.110), calls=%async_computation.2 | async-start | bytes 2097152 | tf_op jit(solution)/shard_map/all_to_all | solution.py:71
  55.2 209.8 %all-gather.3.cloned.1.call-start = ((), (), s32[]{:S(2)}) async-start(), calls=%async_computation.10 | async-start | bytes 3538944 | tf_op jit(solution)/shard_map/all_gather | solution.py:140
  82.3 40.3 %all-to-all-start = ((bf16[64,32,256]{2,0,1:T(8,128)(2,1)}), bf16[64,32,256]{2,0,1:T(8,128)(2,1)}, u32[]{:S(2)}, u32[]{:S(2)}) async-start(bf16[64,32,256]{2,0,1:T(8,128)(2,1)} %bitcast.111), calls=%async_computation | async-start | bytes 2097152 | tf_op jit(solution)/shard_map/all_to_all | solution.py:69
  99.6 18.7 %copy-start.1 = (bf16[2048,2,128]{2,1,0:T(2,128)(2,1)S(1)}, bf16[2048,2,128]{2,1,0:T(2,128)(2,1)}, u32[]{:S(2)}) copy-start(bf16[2048,2,128]{2,1,0:T(2,128)(2,1)} %reshape.159) | copy-start | bytes 3145732
  119.6 7.4 %copy-start.7 = (bf16[8,2,1]{0,1,2:T(2,128)(2,1)}, bf16[8,2,1]{0,1,2:T(2,128)(2,1)S(1)}, u32[]{:S(2)}) copy-start(bf16[8,2,1]{0,1,2:T(2,128)(2,1)S(1)} %copy.159) | copy-start | bytes 100
  226.5 6.7 %copy-start.3 = (f32[2048,2]{0,1:T(2,128)S(1)}, f32[2048,2]{0,1:T(2,128)}, u32[]{:S(2)}) copy-start(f32[2048,2]{0,1:T(2,128)} %get-tuple-element.131) | copy-start | bytes 49156
  244.2 0.7 copy-start.2
  245.6 18.5 %all-to-all-start.4 = ((f32[32,1,256]{2,1,0:T(1,128)}), f32[32,1,256]{2,1,0:T(1,128)}, u32[]{:S(2)}, u32[]{:S(2)}) async-start(f32[32,1,256]{2,1,0:T(1,128)} %broadcast_in_dim.85), calls=%async_computation.4 | async-start | bytes 65536 | tf_op jit(solution)/shard_map/all_to_all | solution.py:26
  255.5 56.2 %reduce-scatter.4.cloned.1.call-start = ((), (), s32[]{:S(2)}) async-start(), calls=%async_computation.11 | async-start | bytes 3538944 | tf_op jit(solution)/shard_map/reduce_scatter | solution.py:35
  269.7 42.3 %copy-start.5 = (s32[8,2]{0,1:T(2,128)S(1)}, s32[8,2]{0,1:T(2,128)}, u32[]{:S(2)}) copy-start(s32[8,2]{0,1:T(2,128)} %param.18) | copy-start | bytes 196
  269.7 65.3 %reduce-scatter.6.cloned.1.call-start = ((), (), s32[]{:S(2)}) async-start(), calls=%async_computation.12 | async-start | bytes 491520 | tf_op jit(solution)/shard_map/reduce_scatter | solution.py:35
  311.7 102.8 %all-gather.5.cloned.1.call-start = ((), (), s32[]{:S(2)}) async-start(), calls=%async_computation.13 | async-start | bytes 7077888 | tf_op jit(solution)/shard_map/all_gather | solution.py:159
  374.1 98.3 %reduce-scatter.8.cloned.1.call-start = ((), (), s32[]{:S(2)}) async-start(), calls=%async_computation.14 | async-start | bytes 7077888 | tf_op jit(solution)/shard_map/reduce_scatter | solution.py:160
  426.6 12.8 %copy-start.6 = (f32[8,2]{0,1:T(2,128)S(1)}, f32[8,2]{0,1:T(2,128)}, u32[]{:S(2)}) copy-start(f32[8,2]{0,1:T(2,128)} %param.19) | copy-start | bytes 196
  429.1 38.7 %all-to-all-start.3 = ((bf16[32,64,256]{2,1,0:T(8,128)(2,1)}), bf16[32,64,256]{2,1,0:T(8,128)(2,1)}, u32[]{:S(2)}, u32[]{:S(2)}) async-start(bf16[32,64,256]{2,1,0:T(8,128)(2,1)} %all_to_all.65), calls=%async_computation.3 | async-start | bytes 2097152 | tf_op jit(solution)/shard_map/all_to_all | solution.py:124
  475.3 31.5 %all-to-all-start.6 = ((bf16[32,2,6144]{2,1,0:T(2,128)(2,1)}), bf16[32,2,6144]{2,1,0:T(2,128)(2,1)}, u32[]{:S(2)}, u32[]{:S(2)}) async-start(bf16[32,2,6144]{2,1,0:T(2,128)(2,1)} %convert_element_type.93), calls=%async_computation.9 | async-start | bytes 1572864 | tf_op jit(solution)/shard_map/all_to_all | solution.py:166
Sparse Core Ops, SparseCore 0:
  57.9 31.4 all-gather.2
  269.8 41.8 reduce-scatter.3
  314.2 20.7 reduce-scatter.5
  374.2 40.2 all-gather.4
  426.7 45.5 reduce-scatter.7
where the time goes:
time: 524 us; the launch traced here: 520 us
  waiting for transfers between devices  196 us (37%)
  local copies, waits for them, and re-layouts  115 us (22%)
  matrix products  54.1 us (10%)
  starting transfers between devices  53.3 us (10%)
  blocking collectives  44.5 us (8%)
  other arithmetic  36.2 us (7%)
  between operations  14 us (3%)
  loops' own time  6.62 us (1%)
    reduce_scatter x2, waiting for transfers between devices, scatter_axes(): x = lax.psum_scatter(x, axis, scatter_dimension=dim, tiled=True)  61.8 us
    dynamic_update_slice x8, local copies, waits for them, and re-layouts, on_device(): lax.map(block_mix, starts).reshape(seg_length, heads_local, head_dim)  52.2 us
    all_gather x1, waiting for transfers between devices, on_device(): gathered = lax.all_gather(arrived, 'seg', axis=0, tiled=True)  40.3 us
    all_to_all x1, blocking collectives, on_device(): lax.all_to_all(outgoing, EP, split_axis=0, concat_axis=0, tiled=True)  30.7 us
    all_to_all x1, waiting for transfers between devices, on_device(): lax.all_to_all(mixture, EP, split_axis=0, concat_axis=1, tiled=True)  28.5 us
    dot_general x4, matrix products, block_mix(): jnp.einsum('hts,she->the', mixing, value_heads, preferred_element_type=jn...  26.3 us
    all_to_all x1, waiting for transfers between devices, on_device(): lax.all_to_all(keys, EP, split_axis=1, concat_axis=0, tiled=True)  25.8 us
    all_to_all x1, waiting for transfers between devices, on_device(): lax.all_to_all(owned_sums.reshape(ep_count, capacity, model_width).astype...  18.8 us
  transfers between devices with their start and end apart: 11, of which 8 were waited for; matrix products, arithmetic and copies ran while one was open for 32% of the time, Pallas kernels for 0%

commit v1 on v0

--- a/solution.py
+++ b/solution.py
@@ -67,7 +67,9 @@
     head_dim = queries.shape[1] // (heads_local * ep_count)
     query_heads, key_heads, value_heads = (
         lax.all_to_all(queries, EP, split_axis=1, concat_axis=0, tiled=True),
-        lax.all_to_all(keys, EP, split_axis=1, concat_axis=0, tiled=True),
+        jnp.concatenate(
+            lax.all_to_all(jnp.stack(jnp.split(keys, lax.axis_size(EP), axis=1)), EP, 0, 0), axis=0
+        ),
         lax.all_to_all(values, EP, split_axis=1, concat_axis=0, tiled=True),
     )
     seg_length = query_heads.shape[0]

time: 524 us -> 545 us (1.040)
  local copies, waits for them, and re-layouts: 115 us -> 156 us
  waiting for transfers between devices: 196 us -> 171 us
    unnamed x23 -> x56, local copies, waits for them, and re-layouts: 7.98 us -> 50.2 us
    all_to_all x1, waiting for transfers between devices: 25.8 us -> 12.8 us  [on_device(): lax.all_to_all(jnp.stack(jnp.split(keys, lax.axis_size(EP), axis=1)), EP,...]
    all_to_all x1, waiting for transfers between devices: 12.2 us -> 0.01 us  [on_device(): lax.all_to_all(values, EP, split_axis=1, concat_axis=0, tiled=True)]
    all_to_all x1, starting transfers between devices: 5.62 us -> 11.8 us  [on_device(): lax.all_to_all(values, EP, split_axis=1, concat_axis=0, tiled=True)]
  transfers between devices with their start and end apart: 11 -> 11, of which waited for: 8 -> 7; matrix products, arithmetic and copies ran while one was open for 32% -> 38% of each run, Pallas kernels for 0% -> 0%
where the time goes in v1:
time: 545 us; the launch traced here: 539 us
  waiting for transfers between devices  171 us (31%)
  local copies, waits for them, and re-layouts  156 us (29%)
  starting transfers between devices  57.5 us (11%)
  matrix products  52.8 us (10%)
  blocking collectives  44.6 us (8%)
  other arithmetic  36.3 us (7%)
  between operations  14 us (3%)
  loops' own time  6.62 us (1%)
    reduce_scatter x2, waiting for transfers between devices, scatter_axes(): x = lax.psum_scatter(x, axis, scatter_dimension=dim, tiled=True)  61.8 us
    dynamic_update_slice x8, local copies, waits for them, and re-layouts, on_device(): lax.map(block_mix, starts).reshape(seg_length, heads_local, head_dim)  52.2 us
    unnamed x56, local copies, waits for them, and re-layouts  50.2 us
    all_gather x1, waiting for transfers between devices, on_device(): gathered = lax.all_gather(arrived, 'seg', axis=0, tiled=True)  40.3 us
    all_to_all x1, blocking collectives, on_device(): lax.all_to_all(outgoing, EP, split_axis=0, concat_axis=0, tiled=True)  30.7 us
    all_to_all x1, waiting for transfers between devices, on_device(): lax.all_to_all(mixture, EP, split_axis=0, concat_axis=1, tiled=True)  28.5 us
    dot_general x4, matrix products, block_mix(): jnp.einsum('hts,she->the', mixing, value_heads, preferred_element_type=jn...  26.3 us
    all_to_all x1, waiting for transfers between devices, on_device(): lax.all_to_all(owned_sums.reshape(ep_count, capacity, model_width).astype...  18.8 us
  transfers between devices with their start and end apart: 11, of which 7 were waited for; matrix products, arithmetic and copies ran while one was open for 38% of the time, Pallas kernels for 0%

profile of v1, /device:TPU:2, one launch (start us, length us, event | category | flops | bytes accessed | tf_op | source)
XLA Modules:
  0.0 539.1 jit_solution(18436154600168060661)
XLA Ops:
  7.2 2.5 copy.189
  9.7 11.8 %all-to-all-start.2 = ((bf16[64,32,256]{2,0,1:T(8,128)(2,1)}), bf16[64,32,256]{2,0,1:T(8,128)(2,1)}, u32[]{:S(2)}, u32[]{:S(2)}) async-start(bf16[64,32,256]{2,0,1:T(8,128)(2,1)} %bitcast.169), calls=%async_computation.2 | async-start | bytes 2097152 | tf_op jit(solution)/shard_map/all_to_all | solution.py:73
  65.0 9.8 %all-to-all-start.1 = ((bf16[32,64,256]{2,1,0:T(8,128)(2,1)}), bf16[32,64,256]{2,1,0:T(8,128)(2,1)}, u32[]{:S(2)}, u32[]{:S(2)}) async-start(bf16[32,64,256]{2,1,0:T(8,128)(2,1)} %constant_dynamic-update-slice_fusion), calls=%async_computation.1 | async-start | bytes 2097152 | tf_op jit(solution)/shard_map/all_to_all | solution.py:71
  83.8 2.3 copy.190
  87.4 2.2 reshape.151
  89.6 12.8 %all-to-all-done.1 = bf16[32,64,256]{2,1,0:T(8,128)(2,1)} async-done(((bf16[32,64,256]{2,1,0:T(8,128)(2,1)}), bf16[32,64,256]{2,1,0:T(8,128)(2,1)}, u32[]{:S(2)}, u32[]{:S(2)}) %all-to-all-start.1) | async-done | bytes 1048608 | tf_op jit(solution)/shard_map/all_to_all | solution.py:71
  102.4 5.6 %all-to-all-start = ((bf16[64,32,256]{2,0,1:T(8,128)(2,1)}), bf16[64,32,256]{2,0,1:T(8,128)(2,1)}, u32[]{:S(2)}, u32[]{:S(2)}) async-start(bf16[64,32,256]{2,0,1:T(8,128)(2,1)} %bitcast.170), calls=%async_computation | async-start | bytes 2097152 | tf_op jit(solution)/shard_map/all_to_all | solution.py:69
  108.1 2.1 reshape_reshape.6
  110.2 5.7 %convert_multiply_fusion.1 = bf16[2048,2,128]{2,1,0:T(2,128)(2,1)S(1)} fusion(bf16[2048,2,128]{2,1,0:T(2,128)(2,1)} %reshape_reshape.6, f32[2048,2]{1,0:T(8,128)} %copy.132), kind=kLoop, calls=%fused_computation.27 | loop fusion | flops 1572864 | bytes 2113536 | tf_op jit(solution)/shard_map/sh,shd,she->hde/dot_general | solution.py:103
  119.7 13.8 %all_gather.9 = bf16[8,2,16385]{2,1,0:T(2,128)(2,1)S(1)} all-gather(bf16[1,2,16385]{2,1,0:T(2,128)(2,1)S(1)} %pad_maximum_fusion), channel_id=1, replica_groups=mesh['seg'=8,'ep_0'=8,'ep_1'=4] {'seg'}, dimensions={0}, use_global_device_ids=true | all-gather | bytes 589860 | tf_op jit(solution)/shard_map/all_gather | solution.py:16
  134.9 2.4 copy.129
  139.3 2.2 reshape.155
  141.5 2.1 reshape.148
  143.7 2.3 copy.128
  146.0 99.4 %while.11 = (s32[]{:T(128)}, f32[4,512,2,128]{1,0,3,2:T(4,128)}, s32[4]{0:T(128)S(1)}, bf16[2048,2,128]{2,0,1:T(8,128)(2,1)}, bf16[2048,2,128]{2,0,1:T(8,128)(2,...) while((s32[]{:T(128)}, f32[4,512,2,128]{1,0,3,2:T(4,128)}, ...), condition=%wide.region_3.4_spmd.clone, body=%wide.region_2.3_spmd.clone.sunk | while | flops 1085276672 | bytes 7110819 | solution.py:98
  151.3 6.6 %fusion.58 = f32[1,512,2,128]{3,1,2,0:T(8,128)} fusion(bf16[2048,2,128]{2,0,1:T(8,128)(2,1)} %get-tuple-element.204, bf16[2048,2,128]{2,0,1:T(8,128)(2,1)} %get-tuple-element.202, f32[2,2048]{1,0:T(2,128)} %get-tuple-element.203, f32[2,512]{1,0:T(2,128)S(1)} %constant_dynamic-slice_fusion.2, pred[512,2048]{1,0:T(8,128)(4,1)} %iota_compare_fusion.5, ...), kind=kOutput, calls=%fused_computation.4.clone.1 | convolution fusion | flops 1084227584 | bytes 3952644 | tf_op jit(solution)/shard_map/while/body/eval_jaxpr/hts,she->the/dot_general | solution.py:96
  157.8 1.9 copy.194
  159.8 11.1 %dynamic_update_slice.6 = f32[4,512,2,128]{1,0,3,2:T(4,128)} dynamic-update-slice(f32[4,512,2,128]{1,0,3,2:T(4,128)} %get-tuple-element.189, f32[1,512,2,128]{1,0,3,2:T(1,128)} %copy.194, s32[]{:T(128)} %get-tuple-element.188, s32[]{:T(128)} %constant.22.clone.1..sunk, s32[]{:T(128)} %constant.22.clone.1..sunk, s32[]{:T(128)} %constant.22.clone.1..sunk) | dynamic-update-slice | bytes 1048580 | tf_op jit(solution)/shard_map/while/body/jit(dynamic_update_index_in_dim)/dynamic_update_slice | solution.py:98
  176.1 6.6 %fusion.58 = f32[1,512,2,128]{3,1,2,0:T(8,128)} fusion(bf16[2048,2,128]{2,0,1:T(8,128)(2,1)} %get-tuple-element.204, bf16[2048,2,128]{2,0,1:T(8,128)(2,1)} %get-tuple-element.202, f32[2,2048]{1,0:T(2,128)} %get-tuple-element.203, f32[2,512]{1,0:T(2,128)S(1)} %constant_dynamic-slice_fusion.2, pred[512,2048]{1,0:T(8,128)(4,1)} %iota_compare_fusion.5, ...), kind=kOutput, calls=%fused_computation.4.clone.1 | convolution fusion | flops 1084227584 | bytes 3952644 | tf_op jit(solution)/shard_map/while/body/eval_jaxpr/hts,she->the/dot_general | solution.py:96
  184.6 11.1 %dynamic_update_slice.6 = f32[4,512,2,128]{1,0,3,2:T(4,128)} dynamic-update-slice(f32[4,512,2,128]{1,0,3,2:T(4,128)} %get-tuple-element.189, f32[1,512,2,128]{1,0,3,2:T(1,128)} %copy.194, s32[]{:T(128)} %get-tuple-element.188, s32[]{:T(128)} %constant.22.clone.1..sunk, s32[]{:T(128)} %constant.22.clone.1..sunk, s32[]{:T(128)} %constant.22.clone.1..sunk) | dynamic-update-slice | bytes 1048580 | tf_op jit(solution)/shard_map/while/body/jit(dynamic_update_index_in_dim)/dynamic_update_slice | solution.py:98
  201.0 6.6 %fusion.58 = f32[1,512,2,128]{3,1,2,0:T(8,128)} fusion(bf16[2048,2,128]{2,0,1:T(8,128)(2,1)} %get-tuple-element.204, bf16[2048,2,128]{2,0,1:T(8,128)(2,1)} %get-tuple-element.202, f32[2,2048]{1,0:T(2,128)} %get-tuple-element.203, f32[2,512]{1,0:T(2,128)S(1)} %constant_dynamic-slice_fusion.2, pred[512,2048]{1,0:T(8,128)(4,1)} %iota_compare_fusion.5, ...), kind=kOutput, calls=%fused_computation.4.clone.1 | convolution fusion | flops 1084227584 | bytes 3952644 | tf_op jit(solution)/shard_map/while/body/eval_jaxpr/hts,she->the/dot_general | solution.py:96
  207.6 1.9 copy.194
  209.5 11.1 %dynamic_update_slice.6 = f32[4,512,2,128]{1,0,3,2:T(4,128)} dynamic-update-slice(f32[4,512,2,128]{1,0,3,2:T(4,128)} %get-tuple-element.189, f32[1,512,2,128]{1,0,3,2:T(1,128)} %copy.194, s32[]{:T(128)} %get-tuple-element.188, s32[]{:T(128)} %constant.22.clone.1..sunk, s32[]{:T(128)} %constant.22.clone.1..sunk, s32[]{:T(128)} %constant.22.clone.1..sunk) | dynamic-update-slice | bytes 1048580 | tf_op jit(solution)/shard_map/while/body/jit(dynamic_update_index_in_dim)/dynamic_update_slice | solution.py:98
  225.8 6.6 %fusion.58 = f32[1,512,2,128]{3,1,2,0:T(8,128)} fusion(bf16[2048,2,128]{2,0,1:T(8,128)(2,1)} %get-tuple-element.204, bf16[2048,2,128]{2,0,1:T(8,128)(2,1)} %get-tuple-element.202, f32[2,2048]{1,0:T(2,128)} %get-tuple-element.203, f32[2,512]{1,0:T(2,128)S(1)} %constant_dynamic-slice_fusion.2, pred[512,2048]{1,0:T(8,128)(4,1)} %iota_compare_fusion.5, ...), kind=kOutput, calls=%fused_computation.4.clone.1 | convolution fusion | flops 1084227584 | bytes 3952644 | tf_op jit(solution)/shard_map/while/body/eval_jaxpr/hts,she->the/dot_general | solution.py:96
  234.3 11.1 %dynamic_update_slice.6 = f32[4,512,2,128]{1,0,3,2:T(4,128)} dynamic-update-slice(f32[4,512,2,128]{1,0,3,2:T(4,128)} %get-tuple-element.189, f32[1,512,2,128]{1,0,3,2:T(1,128)} %copy.194, s32[]{:T(128)} %get-tuple-element.188, s32[]{:T(128)} %constant.22.clone.1..sunk, s32[]{:T(128)} %constant.22.clone.1..sunk, s32[]{:T(128)} %constant.22.clone.1..sunk) | dynamic-update-slice | bytes 1048580 | tf_op jit(solution)/shard_map/while/body/jit(dynamic_update_index_in_dim)/dynamic_update_slice | solution.py:98
  245.5 3.7 reshape.152
  252.1 3.4 fusion.14
  255.5 3.7 copy.138
  259.2 2.5 reshape_reshape.7
  264.6 9.8 %all-to-all-start.4 = ((f32[32,1,256]{2,1,0:T(1,128)}), f32[32,1,256]{2,1,0:T(1,128)}, u32[]{:S(2)}, u32[]{:S(2)}) async-start(f32[32,1,256]{2,1,0:T(1,128)} %broadcast_in_dim.85), calls=%async_computation.4 | async-start | bytes 65536 | tf_op jit(solution)/shard_map/all_to_all | solution.py:26
  275.2 7.8 %all-to-all-done.4 = f32[32,1,256]{2,1,0:T(1,128)} async-done(((f32[32,1,256]{2,1,0:T(1,128)}), f32[32,1,256]{2,1,0:T(1,128)}, u32[]{:S(2)}, u32[]{:S(2)}) %all-to-all-start.4) | async-done | bytes 32800 | tf_op jit(solution)/shard_map/all_to_all | solution.py:26
  283.9 4.7 convolution_convert_fusion.1
  288.7 41.9 %reduce-scatter.4.cloned.1.call-done = bf16[32,6144]{1,0:T(8,128)(2,1)} async-done(((bf16[256,6144]{1,0:T(8,128)(2,1)}), bf16[32,6144]{1,0:T(8,128)(2,1)}) %reduce-scatter.4.cloned.1.call-update) | async-done | bytes 393232 | tf_op jit(solution)/shard_map/reduce_scatter | solution.py:35
  334.1 19.9 %reduce-scatter.6.cloned.1.call-done = bf16[8,6144]{1,0:T(8,128)(2,1)} async-done(((bf16[32,6144]{1,0:T(8,128)(2,1)}), bf16[8,6144]{1,0:T(8,128)(2,1)}) %reduce-scatter.6.cloned.1.call-update) | async-done | bytes 98320 | tf_op jit(solution)/shard_map/reduce_scatter | solution.py:35
  354.0 1.9 convolution_convert_fusion.2
  355.9 2.0 reshape.156
  359.4 30.7 %all_to_all.66 = bf16[32,2,6144]{2,1,0:T(2,128)(2,1)} all-to-all(bf16[32,2,6144]{2,1,0:T(2,128)(2,1)S(1)} %bitcast.171), channel_id=1, replica_groups=mesh['seg'=8,'ep_0'=8,'ep_1'=4] {'ep_0','ep_1'}, dimensions={0} | all-to-all | bytes 1572864 | tf_op jit(solution)/shard_map/all_to_all | solution.py:158
  390.1 3.0 reshape.158
  393.1 40.3 %all-gather.5.cloned.1.call-done = bf16[512,6144]{1,0:T(8,128)(2,1)} async-done(((bf16[64,6144]{1,0:T(8,128)(2,1)}), bf16[512,6144]{1,0:T(8,128)(2,1)}) %all-gather.5.cloned.1.call-update) | async-done | bytes 6291472 | tf_op jit(solution)/shard_map/all_gather | solution.py:161
  433.4 12.0 %convolution_convert_fusion = bf16[512,6144]{1,0:T(8,128)(2,1)} fusion(bf16[1,288,6144]{2,1,0:T(8,128)(2,1)S(1)} %copy-done, bf16[512,6144]{1,0:T(8,128)(2,1)} %all-gather.5.cloned.1.call-done, bf16[1,6144,288]{1,2,0:T(8,128)(2,1)} %param.20), kind=kOutput, calls=%fused_computation.10 | convolution fusion | flops 3627761664 | bytes 19660800 | tf_op jit(solution)/shard_map/dot_general | solution.py:59
  445.5 2.5 all_to_all.54
  448.0 10.2 %all-to-all-start.3 = ((bf16[32,64,256]{2,1,0:T(8,128)(2,1)}), bf16[32,64,256]{2,1,0:T(8,128)(2,1)}, u32[]{:S(2)}, u32[]{:S(2)}) async-start(bf16[32,64,256]{2,1,0:T(8,128)(2,1)} %all_to_all.54), calls=%async_computation.3 | async-start | bytes 2097152 | tf_op jit(solution)/shard_map/all_to_all | solution.py:126
  458.3 28.5 %all-to-all-done.3 = bf16[32,64,256]{2,1,0:T(8,128)(2,1)} async-done(((bf16[32,64,256]{2,1,0:T(8,128)(2,1)}), bf16[32,64,256]{2,1,0:T(8,128)(2,1)}, u32[]{:S(2)}, u32[]{:S(2)}) %all-to-all-start.3) | async-done | bytes 1048608 | tf_op jit(solution)/shard_map/all_to_all | solution.py:126
  491.4 2.9 convert_element_type.93
  494.2 9.8 %all-to-all-start.6 = ((bf16[32,2,6144]{2,1,0:T(2,128)(2,1)}), bf16[32,2,6144]{2,1,0:T(2,128)(2,1)}, u32[]{:S(2)}, u32[]{:S(2)}) async-start(bf16[32,2,6144]{2,1,0:T(2,128)(2,1)} %convert_element_type.93), calls=%async_computation.9 | async-start | bytes 1572864 | tf_op jit(solution)/shard_map/all_to_all | solution.py:168
  504.1 2.8 multiply_convert_fusion.1
  506.9 18.8 %all-to-all-done.6 = bf16[32,2,6144]{2,1,0:T(2,128)(2,1)} async-done(((bf16[32,2,6144]{2,1,0:T(2,128)(2,1)}), bf16[32,2,6144]{2,1,0:T(2,128)(2,1)}, u32[]{:S(2)}, u32[]{:S(2)}) %all-to-all-start.6) | async-done | bytes 786464 | tf_op jit(solution)/shard_map/all_to_all | solution.py:168
  525.7 2.0 convert.7
  (131 shorter events, 101.0 us)
Async XLA Ops:
  7.2 426.3 %copy-start = (bf16[1,288,6144]{2,1,0:T(8,128)(2,1)S(1)}, bf16[1,288,6144]{2,1,0:T(8,128)(2,1)}, u32[]{:S(2)}) copy-start(bf16[1,288,6144]{2,1,0:T(8,128)(2,1)} %param.21) | copy-start | bytes 10616836
  9.7 66.0 %copy-start.5 = (f32[2048,2]{0,1:T(2,128)S(1)}, f32[2048,2]{0,1:T(2,128)}, u32[]{:S(2)}) copy-start(f32[2048,2]{0,1:T(2,128)} %param.15) | copy-start | bytes 49156
  9.7 55.4 %all-to-all-start.2 = ((bf16[64,32,256]{2,0,1:T(8,128)(2,1)}), bf16[64,32,256]{2,0,1:T(8,128)(2,1)}, u32[]{:S(2)}, u32[]{:S(2)}) async-start(bf16[64,32,256]{2,0,1:T(8,128)(2,1)} %bitcast.169), calls=%async_computation.2 | async-start | bytes 2097152 | tf_op jit(solution)/shard_map/all_to_all | solution.py:73
  65.0 37.4 %all-to-all-start.1 = ((bf16[32,64,256]{2,1,0:T(8,128)(2,1)}), bf16[32,64,256]{2,1,0:T(8,128)(2,1)}, u32[]{:S(2)}, u32[]{:S(2)}) async-start(bf16[32,64,256]{2,1,0:T(8,128)(2,1)} %constant_dynamic-update-slice_fusion), calls=%async_computation.1 | async-start | bytes 2097152 | tf_op jit(solution)/shard_map/all_to_all | solution.py:71
  74.9 209.0 %all-gather.3.cloned.1.call-start = ((), (), s32[]{:S(2)}) async-start(), calls=%async_computation.10 | async-start | bytes 3538944 | tf_op jit(solution)/shard_map/all_gather | solution.py:142
  102.4 39.1 %all-to-all-start = ((bf16[64,32,256]{2,0,1:T(8,128)(2,1)}), bf16[64,32,256]{2,0,1:T(8,128)(2,1)}, u32[]{:S(2)}, u32[]{:S(2)}) async-start(bf16[64,32,256]{2,0,1:T(8,128)(2,1)} %bitcast.170), calls=%async_computation | async-start | bytes 2097152 | tf_op jit(solution)/shard_map/all_to_all | solution.py:69
  110.2 5.7 %copy-start.1 = (bf16[2048,2,128]{2,1,0:T(2,128)(2,1)S(1)}, bf16[2048,2,128]{2,1,0:T(2,128)(2,1)}, u32[]{:S(2)}) copy-start(bf16[2048,2,128]{2,1,0:T(2,128)(2,1)} %reshape.151) | copy-start | bytes 3145732
  118.6 18.7 %copy-start.2 = (bf16[2048,2,128]{2,1,0:T(2,128)(2,1)S(1)}, bf16[2048,2,128]{2,1,0:T(2,128)(2,1)}, u32[]{:S(2)}) copy-start(bf16[2048,2,128]{2,1,0:T(2,128)(2,1)} %reshape.151) | copy-start | bytes 3145732
  138.6 7.4 %copy-start.8 = (bf16[8,2,1]{0,1,2:T(2,128)(2,1)}, bf16[8,2,1]{0,1,2:T(2,128)(2,1)S(1)}, u32[]{:S(2)}) copy-start(bf16[8,2,1]{0,1,2:T(2,128)(2,1)S(1)} %copy.152) | copy-start | bytes 100
  245.5 6.7 %copy-start.4 = (f32[2048,2]{0,1:T(2,128)S(1)}, f32[2048,2]{0,1:T(2,128)}, u32[]{:S(2)}) copy-start(f32[2048,2]{0,1:T(2,128)} %get-tuple-element.131) | copy-start | bytes 49156
  263.1 0.7 copy-start.3
  264.6 18.5 %all-to-all-start.4 = ((f32[32,1,256]{2,1,0:T(1,128)}), f32[32,1,256]{2,1,0:T(1,128)}, u32[]{:S(2)}, u32[]{:S(2)}) async-start(f32[32,1,256]{2,1,0:T(1,128)} %broadcast_in_dim.85), calls=%async_computation.4 | async-start | bytes 65536 | tf_op jit(solution)/shard_map/all_to_all | solution.py:26
  274.4 56.2 %reduce-scatter.4.cloned.1.call-start = ((), (), s32[]{:S(2)}) async-start(), calls=%async_computation.11 | async-start | bytes 3538944 | tf_op jit(solution)/shard_map/reduce_scatter | solution.py:35
  288.6 42.3 %copy-start.6 = (s32[8,2]{0,1:T(2,128)S(1)}, s32[8,2]{0,1:T(2,128)}, u32[]{:S(2)}) copy-start(s32[8,2]{0,1:T(2,128)} %param.18) | copy-start | bytes 196
  288.7 65.3 %reduce-scatter.6.cloned.1.call-start = ((), (), s32[]{:S(2)}) async-start(), calls=%async_computation.12 | async-start | bytes 491520 | tf_op jit(solution)/shard_map/reduce_scatter | solution.py:35
  330.7 102.8 %all-gather.5.cloned.1.call-start = ((), (), s32[]{:S(2)}) async-start(), calls=%async_computation.13 | async-start | bytes 7077888 | tf_op jit(solution)/shard_map/all_gather | solution.py:161
  393.1 98.3 %reduce-scatter.8.cloned.1.call-start = ((), (), s32[]{:S(2)}) async-start(), calls=%async_computation.14 | async-start | bytes 7077888 | tf_op jit(solution)/shard_map/reduce_scatter | solution.py:162
  445.5 12.8 %copy-start.7 = (f32[8,2]{0,1:T(2,128)S(1)}, f32[8,2]{0,1:T(2,128)}, u32[]{:S(2)}) copy-start(f32[8,2]{0,1:T(2,128)} %param.19) | copy-start | bytes 196
  448.0 38.7 %all-to-all-start.3 = ((bf16[32,64,256]{2,1,0:T(8,128)(2,1)}), bf16[32,64,256]{2,1,0:T(8,128)(2,1)}, u32[]{:S(2)}, u32[]{:S(2)}) async-start(bf16[32,64,256]{2,1,0:T(8,128)(2,1)} %all_to_all.54), calls=%async_computation.3 | async-start | bytes 2097152 | tf_op jit(solution)/shard_map/all_to_all | solution.py:126
  494.2 31.5 %all-to-all-start.6 = ((bf16[32,2,6144]{2,1,0:T(2,128)(2,1)}), bf16[32,2,6144]{2,1,0:T(2,128)(2,1)}, u32[]{:S(2)}, u32[]{:S(2)}) async-start(bf16[32,2,6144]{2,1,0:T(2,128)(2,1)} %convert_element_type.93), calls=%async_computation.9 | async-start | bytes 1572864 | tf_op jit(solution)/shard_map/all_to_all | solution.py:168
Sparse Core Ops, SparseCore 0:
  77.6 31.4 all-gather.2
  288.8 41.8 reduce-scatter.3
  333.2 20.7 reduce-scatter.5
  393.2 40.1 all-gather.4
  445.6 45.5 reduce-scatter.7
